TPU v7x, 512 devices: a whole 4x8x8 slice. The times are simulated.
512 devices in a mesh: dp: 128 (over y, z, core), mp: 4 (over x).
Axes of the slice: x: 4, y: 8, z: 8, core: 2. Of those that a mesh axis runs over, the one named last changes fastest.
Arguments:
- grad_cot: bfloat16 [131072, 2048], P('dp', 'mp'), may hold values from -0.1875 to 0.1875
- grad_hidden: bfloat16 [131072, 1024], P('dp'), may hold values from -6 to 6
- old_place: int32 [128], replicated, may hold values from 0 to 31
- master: float32 [32, 4, 524288], P(None, 'mp', 'dp'), may hold values from -0.125 to 0.125
- moment_one: float32 [32, 4, 524288], P(None, 'mp', 'dp'), may hold values from -2 to 2
- moment_two: float32 [32, 4, 524288], P(None, 'mp', 'dp'), may hold values from 0.05 to 1
- new_place: int32 [128], replicated, may hold values from 0 to 31
- rows: bfloat16 [16384, 2048], P('dp', 'mp'), may hold values from -6 to 6
- dest: int32 [16384], P('dp'), may hold values from 0 to 127, as said below
- counts: int32 [128], P('dp'), may hold values from 112 to 128, as said below
Outputs:
- master_new: float32 [32, 4, 524288], P(None, 'mp', 'dp')
- moment_one_new: float32 [32, 4, 524288], P(None, 'mp', 'dp')
- moment_two_new: float32 [32, 4, 524288], P(None, 'mp', 'dp')
- projected: bfloat16 [16384, 1024], P('dp', 'mp')
Inputs may be any that keep to these rules, and one draw needn't show every extreme that they name: `dest`: each token shard's 128 rows name exactly 64 distinct replica groups, 2 rows each, so no replica group receives more than 2 rows from one shard; in every draw one replica group is named by 2 rows of every shard. `counts`: some shard is full and some shard has the fewest live rows allowed.
All inputs are finite; a program needn't handle non-finite values.
Results may differ from a plain program's by a relative error of at most 0.005.
Values may be sent and summed in bfloat16 or wider, within the bound.
A program may use at most 64 MiB of HBM per device.

v0:
```python
import jax
import jax.numpy as jnp
from jax import lax
from jax.sharding import PartitionSpec as P

beta_first = 0.9
beta_second = 0.95
learn_rate = 0.01
decay_rate = 0.1
adam_eps = 1e-08
bias_first = 1.0 - 0.9**10
bias_second = 1.0 - 0.95**10


def adam_update(gradient, master, moment_one, moment_two):
    first_new = beta_first * moment_one + (1.0 - beta_first) * gradient
    second_new = beta_second * moment_two + (1.0 - beta_second) * gradient * gradient
    step_dir = first_new / bias_first / (jnp.sqrt(second_new / bias_second) + adam_eps)
    updated = master - learn_rate * (step_dir + decay_rate * master)
    return (updated, first_new, second_new)


def body(
    grad_cot, grad_hidden, old_place, master, moment_one, moment_two, new_place, rows, dest, counts
):
    replicas = lax.axis_size("dp")
    experts = master.shape[0]
    slab_rows = grad_cot.shape[1]
    hidden_units = grad_hidden.shape[1]
    share_size = master.shape[2]
    partial_value = lax.dot_general(
        grad_cot, grad_hidden, (((0,), (0,)), ((), ())), preferred_element_type=jnp.float32
    )
    pieces = partial_value.reshape(replicas, share_size)
    arrived = lax.all_to_all(pieces, "dp", split_axis=0, concat_axis=0, tiled=True)
    expert_ids = jnp.arange(experts, dtype=jnp.int32)
    owner_of = (old_place[None, :] == expert_ids[:, None]).astype(jnp.float32)
    gradient = jnp.dot(
        owner_of, arrived, precision=lax.Precision.HIGHEST, preferred_element_type=jnp.float32
    )
    updated, first_new, second_new = adam_update(
        gradient, master[:, 0, :], moment_one[:, 0, :], moment_two[:, 0, :]
    )
    low_copy = updated.astype(jnp.bfloat16)
    chooser = (new_place[:, None] == expert_ids[None, :]).astype(jnp.bfloat16)
    outgoing = jnp.dot(chooser, low_copy, preferred_element_type=jnp.float32).astype(jnp.bfloat16)
    incoming = lax.all_to_all(outgoing, "dp", split_axis=0, concat_axis=0, tiled=True)
    weight_slab = incoming.reshape(slab_rows, hidden_units)
    local_rows = rows.shape[0]
    capacity = local_rows * 2 // replicas
    row_live = jnp.arange(local_rows, dtype=jnp.int32) < counts[0]
    target = (dest[:, None] == jnp.arange(replicas, dtype=jnp.int32)[None, :]).astype(jnp.int32)
    before = jnp.cumsum(target, axis=0) - target
    rank_within = jnp.sum(before * target, axis=1)
    slot_index = dest * capacity + rank_within
    sent_rows = jnp.where(row_live[:, None], rows, jnp.zeros((), jnp.bfloat16))
    buffer = jnp.zeros((replicas * capacity, slab_rows), jnp.bfloat16).at[slot_index].set(sent_rows)
    partial_out = jnp.einsum(
        "pcd,df->pcf",
        lax.all_to_all(
            buffer.reshape(replicas, capacity, slab_rows),
            "dp",
            split_axis=0,
            concat_axis=0,
            tiled=True,
        ),
        weight_slab,
        preferred_element_type=jnp.float32,
    )
    summed = lax.psum_scatter(partial_out, "mp", scatter_dimension=2, tiled=True)
    returned = lax.all_to_all(
        summed.astype(jnp.bfloat16), "dp", split_axis=0, concat_axis=0, tiled=True
    )
    flat_rows = returned.reshape(replicas * capacity, returned.shape[2])
    gathered = flat_rows[slot_index]
    projected = jnp.where(row_live[:, None], gathered, jnp.zeros((), jnp.bfloat16))
    return (updated[:, None, :], first_new[:, None, :], second_new[:, None, :], projected)


def solution(mesh):
    return jax.shard_map(
        body,
        mesh=mesh,
        in_specs=(
            P("dp", "mp"),
            P("dp", None),
            P(),
            P(None, "mp", "dp"),
            P(None, "mp", "dp"),
            P(None, "mp", "dp"),
            P(),
            P("dp", "mp"),
            P("dp"),
            P("dp"),
        ),
        out_specs=(P(None, "mp", "dp"), P(None, "mp", "dp"), P(None, "mp", "dp"), P("dp", "mp")),
        check_vma=False,
    )
```

profile of v0, /device:TPU:1, one launch (start us, length us, event | category | flops | bytes accessed | tf_op | source)
XLA Modules:
  0.0 233.7 jit_solution(17920196418825044128)
XLA Ops:
  7.2 1.6 copy-done
  8.8 3.8 %fusion.22 = f32[512,1024]{1,0:T(8,128)} fusion(bf16[1024,512]{1,0:T(8,128)(2,1)} %param.10, bf16[1024,1024]{1,0:T(8,128)(2,1)S(1)} %copy-done), kind=kOutput, calls=%fused_computation.37 | convolution fusion | flops 1073741824 | bytes 5242880 | tf_op jit(solution)/shard_map/dot_general | solution.py:31
  12.6 4.7 %all_to_all.27 = f32[128,1,4096]{2,1,0:T(1,128)} reshape(f32[512,1024]{1,0:T(8,128)} %fusion.22) | data formatting | bytes 4194304 | tf_op jit(solution)/shard_map/all_to_all | solution.py:35
  17.3 70.7 %all_to_all.32 = f32[128,1,4096]{2,1,0:T(1,128)S(1)} all-to-all(f32[128,1,4096]{2,1,0:T(1,128)} %all_to_all.27), channel_id=1, replica_groups=mesh['dp'=128,'mp'=4] {'dp'}, dimensions={0} | all-to-all | bytes 4194304 | tf_op jit(solution)/shard_map/all_to_all | solution.py:35
  88.0 3.8 %fusion.15 = (f32[32,1,4096]{2,0,1:T(8,128)S(1)}, f32[32,4096]{1,0:T(8,128)S(1)}, f32[32,1,4096]{2,0,1:T(8,128)}) fusion(f32[32,1,4096]{2,1,0:T(1,128)S(1)} %copy-done.1, f32[32,1,4096]{2,1,0:T(1,128)S(1)} %copy-done.2, f32[32,1,4096]{2,1,0:T(1,128)S(1)} %copy-done.3, f32[128,1,4096]{2,1,0:T(1,128)S(1)} %all_to_all.32, s32[128]{0:T(128)S(1)} %copy-done.7), kind=kOutput, calls=%fused_computation.24 | convolution fusion | flops 203296768 | bytes 5243392 | tf_op jit(solution)/shard_map/dot_general | solution.py:38
  91.9 1.5 fusion
  93.9 3.3 %reduce.1 = bf16[128,4096]{1,0:T(8,128)(2,1)} reduce(bf16[128,1,4096]{2,0,1:T(8,128)(2,1)} %fusion, bf16[]{:T(256)} %broadcast.43), dimensions={1}, to_apply=%copy.38.reduce_sub_computation | reduce | bytes 2097154 | tf_op jit(solution)/shard_map/all_to_all | solution.py:47
  97.2 2.7 %reshape.61 = bf16[128,2,2048]{2,1,0:T(2,128)(2,1)} reshape(bf16[128,4096]{1,0:T(8,128)(2,1)} %reduce.1) | data formatting | bytes 2097152
  99.9 8.2 %all-to-all-start.2 = ((bf16[128,2,2048]{2,1,0:T(2,128)(2,1)}), bf16[128,2,2048]{2,1,0:T(2,128)(2,1)}, u32[]{:S(2)}, u32[]{:S(2)}) async-start(bf16[128,2,2048]{2,1,0:T(2,128)(2,1)} %reshape.61), calls=%async_computation.2 | async-start | bytes 2097152 | tf_op jit(solution)/shard_map/all_to_all | solution.py:47
  109.2 1.2 scatter_custom_fusion
  111.2 27.0 %all-to-all-done.2 = bf16[128,2,2048]{2,1,0:T(2,128)(2,1)} async-done(((bf16[128,2,2048]{2,1,0:T(2,128)(2,1)}), bf16[128,2,2048]{2,1,0:T(2,128)(2,1)}, u32[]{:S(2)}, u32[]{:S(2)}) %all-to-all-start.2) | async-done | bytes 1048608 | tf_op jit(solution)/shard_map/all_to_all | solution.py:47
  138.2 7.2 %all-to-all-start.1 = ((bf16[128,2,512]{2,1,0:T(2,128)(2,1)}), bf16[128,2,512]{2,1,0:T(2,128)(2,1)S(1)}, u32[]{:S(2)}, u32[]{:S(2)}) async-start(bf16[128,2,512]{2,1,0:T(2,128)(2,1)} %reshape.35), calls=%async_computation.1 | async-start | bytes 524288 | tf_op jit(solution)/shard_map/all_to_all | solution.py:60
  145.4 7.5 %reshape.62 = bf16[128,1,4096]{2,1,0:T(2,128)(2,1)} reshape(bf16[128,2,2048]{2,1,0:T(2,128)(2,1)} %all-to-all-done.2) | data formatting | bytes 2097152
  152.9 8.7 %reduce = bf16[128,4096]{1,0:T(8,128)(2,1)} reduce(bf16[128,1,4096]{2,1,0:T(2,128)(2,1)} %reshape.62, bf16[]{:T(256)} %constant.36), dimensions={1}, to_apply=%all_to_all.25.reduce_sub_computation | reduce | bytes 2097154 | tf_op jit(solution)/shard_map/all_to_all | solution.py:47
  161.6 2.5 %reshape.56 = bf16[512,1024,1]{1,0,2:T(8,128)(2,1)} reshape(bf16[128,4096]{1,0:T(8,128)(2,1)} %reduce) | data formatting | bytes 2097152 | tf_op jit(solution)/shard_map/reshape | solution.py:48
  164.1 2.7 %fusion.7 = f32[128,2,1024]{2,0,1:T(8,128)} fusion(bf16[512,1024,1]{1,0,2:T(8,128)(2,1)} %reshape.56, bf16[128,2,512]{2,1,0:T(2,128)(2,1)S(1)} %all-to-all-done.1), kind=kOutput, calls=%fused_computation.16 | convolution fusion | flops 268435456 | bytes 2359296 | tf_op jit(solution)/shard_map/pcd,df->pcf/dot_general | solution.py:58
  166.8 28.7 %reduce-scatter.2.cloned.1.call-done = f32[128,2,256]{2,0,1:T(8,128)} async-done(((f32[128,2,1024]{2,0,1:T(8,128)}), f32[128,2,256]{2,0,1:T(8,128)}) %reduce-scatter.2.cloned.1.call-update) | async-done | bytes 262160 | tf_op jit(solution)/shard_map/reduce_scatter | solution.py:70
  195.5 1.0 convert_element_type.17
  197.2 15.7 %all-to-all-start.3 = ((bf16[128,2,256]{2,1,0:T(2,128)(2,1)}), bf16[128,2,256]{2,1,0:T(2,128)(2,1)S(1)}, u32[]{:S(2)}, u32[]{:S(2)}) async-start(bf16[128,2,256]{2,1,0:T(2,128)(2,1)} %copy.40), calls=%async_computation.4 | async-start | bytes 262144 | tf_op jit(solution)/shard_map/all_to_all | solution.py:71
  213.0 1.3 copy.41
  214.3 2.4 %copy.42 = f32[32,1,4096]{2,1,0:T(1,128)} copy(f32[32,1,4096]{2,0,1:T(8,128)} %get-tuple-element.22) | data formatting | bytes 1048576
  216.7 1.3 copy.43
  218.0 7.2 %all-to-all-done.3 = bf16[128,2,256]{2,1,0:T(2,128)(2,1)S(1)} async-done(((bf16[128,2,256]{2,1,0:T(2,128)(2,1)}), bf16[128,2,256]{2,1,0:T(2,128)(2,1)S(1)}, u32[]{:S(2)}, u32[]{:S(2)}) %all-to-all-start.3) | async-done | bytes 131104 | tf_op jit(solution)/shard_map/all_to_all | solution.py:71
  225.3 0.8 gather_fusion
  (29 shorter events, 3.4 us)
Async XLA Ops:
  7.2 1.6 copy-start
  17.3 70.7 %copy-start.1 = (f32[32,1,4096]{2,1,0:T(1,128)S(1)}, f32[32,1,4096]{2,1,0:T(1,128)}, u32[]{:S(2)}) copy-start(f32[32,1,4096]{2,1,0:T(1,128)} %param.15) | copy-start | bytes 1572868
  17.3 70.7 %copy-start.2 = (f32[32,1,4096]{2,1,0:T(1,128)S(1)}, f32[32,1,4096]{2,1,0:T(1,128)}, u32[]{:S(2)}) copy-start(f32[32,1,4096]{2,1,0:T(1,128)} %param.14) | copy-start | bytes 1572868
  17.3 70.7 %copy-start.3 = (f32[32,1,4096]{2,1,0:T(1,128)S(1)}, f32[32,1,4096]{2,1,0:T(1,128)}, u32[]{:S(2)}) copy-start(f32[32,1,4096]{2,1,0:T(1,128)} %param.13) | copy-start | bytes 1572868
  17.3 70.7 %copy-start.7 = (s32[128]{0:T(128)S(1)}, s32[128]{0:T(128)}, u32[]{:S(2)}) copy-start(s32[128]{0:T(128)} %param.12) | copy-start | bytes 1540
  88.0 3.9 %copy-start.6 = (s32[128]{0:T(128)S(1)}, s32[128]{0:T(128)}, u32[]{:S(2)}) copy-start(s32[128]{0:T(128)} %param.16) | copy-start | bytes 1540
  97.2 11.5 %copy-start.5 = (s32[128]{0:T(128)S(1)}, s32[128]{0:T(128)}, u32[]{:S(2)}) copy-start(s32[128]{0:T(128)} %param.18) | copy-start | bytes 1540
  97.2 12.0 %copy-start.4 = (bf16[128,512]{1,0:T(8,128)(2,1)S(1)}, bf16[128,512]{1,0:T(8,128)(2,1)}, u32[]{:S(2)}) copy-start(bf16[128,512]{1,0:T(8,128)(2,1)} %param.17) | copy-start | bytes 393220
  99.9 38.3 %all-to-all-start.2 = ((bf16[128,2,2048]{2,1,0:T(2,128)(2,1)}), bf16[128,2,2048]{2,1,0:T(2,128)(2,1)}, u32[]{:S(2)}, u32[]{:S(2)}) async-start(bf16[128,2,2048]{2,1,0:T(2,128)(2,1)} %reshape.61), calls=%async_computation.2 | async-start | bytes 2097152 | tf_op jit(solution)/shard_map/all_to_all | solution.py:47
  138.2 25.9 %all-to-all-start.1 = ((bf16[128,2,512]{2,1,0:T(2,128)(2,1)}), bf16[128,2,512]{2,1,0:T(2,128)(2,1)S(1)}, u32[]{:S(2)}, u32[]{:S(2)}) async-start(bf16[128,2,512]{2,1,0:T(2,128)(2,1)} %reshape.35), calls=%async_computation.1 | async-start | bytes 524288 | tf_op jit(solution)/shard_map/all_to_all | solution.py:60
  145.4 50.1 %reduce-scatter.2.cloned.1.call-start = ((), (), s32[]{:S(2)}) async-start(), calls=%async_computation.5 | async-start | bytes 1310720 | tf_op jit(solution)/shard_map/reduce_scatter | solution.py:70
  197.2 28.0 %all-to-all-start.3 = ((bf16[128,2,256]{2,1,0:T(2,128)(2,1)}), bf16[128,2,256]{2,1,0:T(2,128)(2,1)S(1)}, u32[]{:S(2)}, u32[]{:S(2)}) async-start(bf16[128,2,256]{2,1,0:T(2,128)(2,1)} %copy.40), calls=%async_computation.4 | async-start | bytes 262144 | tf_op jit(solution)/shard_map/all_to_all | solution.py:71
Sparse Core Ops, SparseCore 0:
  167.0 28.5 reduce-scatter.1
where the time goes:
time: 235 us; the launch traced here: 234 us
  blocking collectives  70.7 us (30%)
  waiting for transfers between devices  62.9 us (27%)
  starting transfers between devices  31.1 us (13%)
  local copies, waits for them, and re-layouts  27 us (11%)
  other arithmetic  15.4 us (7%)
  between operations  14.8 us (6%)
  matrix products  11.9 us (5%)
    all_to_all x1, blocking collectives, body(): lax.all_to_all(pieces, 'dp', split_axis=0, concat_axis=0, tiled=True)  70.7 us
    reduce_scatter x1, waiting for transfers between devices, body(): lax.psum_scatter(partial_out, 'mp', scatter_dimension=2, tiled=True)  28.7 us
    all_to_all x1, waiting for transfers between devices, body(): lax.all_to_all(outgoing, 'dp', split_axis=0, concat_axis=0, tiled=True)  27 us
    unnamed x21, local copies, waits for them, and re-layouts  16.8 us
    all_to_all x1, starting transfers between devices, body(): lax.all_to_all(summed.astype(jnp.bfloat16), 'dp', split_axis=0, concat_ax...  15.7 us
    all_to_all x2, other arithmetic, body(): lax.all_to_all(outgoing, 'dp', split_axis=0, concat_axis=0, tiled=True)  12 us
    all_to_all x1, starting transfers between devices, body(): lax.all_to_all(outgoing, 'dp', split_axis=0, concat_axis=0, tiled=True)  8.18 us
    all_to_all x1, waiting for transfers between devices, body(): lax.all_to_all(summed.astype(jnp.bfloat16), 'dp', split_axis=0, concat_ax...  7.21 us
  transfers between devices with their start and end apart: 4, of which 3 were waited for; matrix products, arithmetic and copies ran while one was open for 11% of the time, Pallas kernels for 0%

commit v1 on v0

v1 whole, which is shorter than its diff:
```python
import jax
import jax.numpy as jnp
from jax import lax
from jax.experimental import pallas as pl
from jax.experimental.pallas import tpu as pltpu
from jax.sharding import PartitionSpec as P

MESH = pl.DeviceIdType.MESH
BF = jnp.bfloat16
F32 = jnp.float32
I32 = jnp.int32

NY = 8
NU = 16
NX = 4
EXPERTS = 32

beta_first = 0.9
beta_second = 0.95
learn_rate = 0.01
decay_rate = 0.1
adam_eps = 1e-08
bias_first = 1.0 - 0.9**10
bias_second = 1.0 - 0.95**10


def adam_update(gradient, master, moment_one, moment_two):
    first_new = beta_first * moment_one + (1.0 - beta_first) * gradient
    second_new = beta_second * moment_two + (1.0 - beta_second) * gradient * gradient
    step_dir = first_new / bias_first / (jnp.sqrt(second_new / bias_second) + adam_eps)
    updated = master - learn_rate * (step_dir + decay_rate * master)
    return (updated, first_new, second_new)


def mm(a, b):
    return jnp.dot(a, b, preferred_element_type=F32)


def ones_where(cond):
    return jnp.where(cond, 1.0, 0.0).astype(BF)


def iota(shape, dim):
    return lax.broadcasted_iota(I32, shape, dim)


def swap_index(r, inner_bits, outer_bits, low_bits):
    low = r & ((1 << low_bits) - 1)
    outer = (r >> low_bits) & ((1 << outer_bits) - 1)
    inner = r >> (low_bits + outer_bits)
    return (((outer << inner_bits) | inner) << low_bits) | low


def reorder(first_bits, second_bits, low_bits):
    n = 1 << (first_bits + second_bits + low_bits)
    source = swap_index(iota((n, n), 0), second_bits, first_bits, low_bits)
    return ones_where(iota((n, n), 1) == source)


def kernel(
    cot_h, hid_h, old_ref, mas_h, one_h, two_h, new_s, rows_h, dest_ref, counts_s,
    mas_o, one_o, two_o, proj_o,
    cot, hid, rows, mas, one, two, mas_n, one_n, two_n, proj,
    p_a, p_at, p_c, p_ct, p_s, p_st, own_a, own_b, slots, slots_u,
    row1, row1r, row2, row2r, rowx, rowp,
    ga1, ga1r, ga2, ga2r, gb0, gb1, gb1r, gb2, gb2r,
    wa, wb, xa, xb, ya, yb, oa1, ob1, wa1r, wb1r, wa2r, wb2r,
    ta1, tb1, ta1r, tb1r, ta2, tb2, ta2r, tb2r,
    in_sem, out_sem, loc_sem, snd_sem, rcv_sem,
):
    me = lax.axis_index("dp")
    mp = lax.axis_index("mp")
    y = me // NU
    u = lax.rem(me, NU)

    def peer_y(k):
        t = lax.rem(y + k, NY)
        return t, (t * NU + u, mp)

    def peer_u(k):
        t = lax.rem(u + k, NU)
        return t, (y * NU + t, mp)

    def peer_x(k):
        t = lax.rem(mp + k, NX)
        return t, (me, t)

    rings = {"y": (NY, y, peer_y), "u": (NU, u, peer_u), "x": (NX, mp, peer_x)}

    ins = [(cot_h, cot), (hid_h, hid), (rows_h, rows), (mas_h, mas), (one_h, one), (two_h, two)]
    in_copies = [pltpu.make_async_copy(s, d, in_sem.at[i]) for i, (s, d) in enumerate(ins)]
    for i in (2, 0, 1, 3, 4, 5):
        in_copies[i].start()

    barrier = pltpu.get_barrier_semaphore()
    for n, _, peer in rings.values():

        @pl.loop(1, n)
        def _(k):
            pl.semaphore_signal(barrier, inc=1, device_id=peer(k)[1], device_id_type=MESH)

    def stage(i, ring, src, part, dst, place):
        n, mine, peer = rings[ring]

        def start():
            @pl.loop(1, n)
            def _(k):
                t, device = peer(k)
                pltpu.make_async_remote_copy(
                    src_ref=part(src, t), dst_ref=place(dst, mine), send_sem=snd_sem.at[i],
                    recv_sem=rcv_sem.at[i], device_id=device, device_id_type=MESH,
                ).start()

            pltpu.make_async_copy(part(src, mine), place(dst, mine), loc_sem.at[i]).start()

        return start

    def finish(i, ring, src_all, dst_all, src, part, dst, place):
        n, mine, peer = rings[ring]
        pltpu.make_async_copy(part(src, mine), place(dst, mine), loc_sem.at[i]).wait()
        whole = pltpu.make_async_remote_copy(
            src_ref=src_all(src, n - 1), dst_ref=dst_all(dst, n - 1), send_sem=snd_sem.at[i],
            recv_sem=rcv_sem.at[i], device_id=peer(1)[1], device_id_type=MESH,
        )
        whole.wait_recv()
        return whole

    lead = lambda ref, t: ref.at[t]
    lead_n = lambda ref, n: ref.at[pl.ds(0, n)]
    second = lambda ref, t: ref.at[:, t]
    second_n = lambda ref, n: ref.at[:, pl.ds(0, n)]
    whole_ref = lambda ref, t: ref

    def exchange(i, ring, src, dst, part=lead, place=lead):
        src_all = second_n if part is second else lead_n
        dst_all = second_n if place is second else lead_n
        if part is whole_ref:
            src_all = lambda ref, n: dst_all(dst, n)
        start = stage(i, ring, src, part, dst, place)
        wait = lambda: finish(i, ring, src_all, dst_all, src, part, dst, place)
        return start, wait

    rows1 = exchange(0, "y", row1, row1r)
    rows2 = exchange(1, "u", row2, row2r)
    rowsx = exchange(2, "x", row2r, rowx, part=whole_ref)
    grad_a1 = exchange(3, "y", ga1, ga1r)
    grad_a2 = exchange(4, "u", ga2, ga2r)
    grad_b1 = exchange(5, "u", gb1, gb1r)
    grad_b2 = exchange(6, "y", gb2, gb2r)
    cross_a = exchange(7, "x", wa, xa)
    cross_b = exchange(8, "x", wb, xb)
    weight_a1 = exchange(9, "u", oa1, wa1r, part=second)
    weight_a2 = exchange(10, "y", wa1r, wa2r, part=second)
    weight_b1 = exchange(11, "y", ob1, wb1r)
    weight_b2 = exchange(12, "u", wb1r, wb2r, part=second, place=second)
    back_a1 = exchange(13, "u", ta1, ta1r)
    back_a2 = exchange(14, "y", ta2, ta2r)
    back_b1 = exchange(15, "y", tb1, tb1r)
    back_b2 = exchange(16, "u", tb2, tb2r)
    sent = []

    dest = jnp.broadcast_to(dest_ref[...], (128, 128))
    dest_t = dest.astype(F32).T.astype(I32)
    earlier = (dest == dest_t) & (iota((128, 128), 0) < iota((128, 128), 1))
    rank = jnp.sum(jnp.where(earlier, 1, 0), axis=0, keepdims=True)
    dest_row = dest_ref[...]
    live = iota((1, 128), 1) < counts_s[0]
    slot_y = jnp.where(live, dest_row * 2 + rank, -1)
    slot_u = jnp.where(live, (dest_row & 15) * 16 + (dest_row >> 4) * 2 + rank, -1)
    slots[...] = ones_where(iota((256, 128), 0) == jnp.broadcast_to(slot_y, (256, 128)))
    slots_u[...] = ones_where(iota((256, 128), 0) == jnp.broadcast_to(slot_u, (256, 128)))
    in_copies[2].wait()
    row1[...] = mm(slots[...], rows[...]).astype(BF).reshape(NY, 32, 512)

    p_a[...] = reorder(3, 4, 2)

    pl.semaphore_wait(barrier, NY - 1 + NU - 1 + NX - 1)
    rows1[0]()

    in_copies[0].wait()
    in_copies[1].wait()

    @pl.loop(0, NX)
    def _(b):
        at = pl.multiple_of(b * 256, 256)
        to = pl.multiple_of(b * 128, 128)
        part = lax.dot_general(
            cot[...], hid[:, pl.ds(at, 256)], (((0,), (0,)), ((), ())), preferred_element_type=F32
        ).astype(BF)
        ga1[:, :, pl.ds(to, 128)] = part[:, :128].reshape(NY, 64, 128)
        gb0[:, pl.ds(to, 128)] = part[:, 128:]

    grad_a1[0]()
    gb1[...] = mm(p_a[...], gb0[...]).astype(BF).reshape(NU, 32, 512)
    grad_b1[0]()

    p_at[...] = reorder(4, 3, 2)
    p_s[...] = reorder(3, 4, 1)
    p_st[...] = reorder(4, 3, 1)
    p_c[...] = reorder(2, 5, 2)
    p_ct[...] = reorder(5, 2, 2)
    old = jnp.broadcast_to(old_ref[...], (8, 128)).astype(F32).astype(BF)
    spread_b = ones_where(iota((128, 512), 0) == (iota((128, 512), 1) >> 2))
    col = iota((128, 512), 1)
    spread_a = ones_where(iota((128, 512), 0) == (((col >> 2) & 7) * NU + (col >> 5)))
    for spread, own in ((spread_a, own_a), (spread_b, own_b)):
        holder = mm(old, spread)[0:1].astype(I32)
        wanted = holder * 4 + (iota((1, 512), 1) & 3)
        own[...] = ones_where(iota((128, 512), 0) == jnp.broadcast_to(wanted, (128, 512)))

    sent.append(rows1[1]())
    row2[...] = mm(p_s[...], row1r[...].reshape(256, 512)).astype(BF).reshape(NU, 16, 512)

    sent.append(grad_a1[1]())
    ga2[...] = mm(p_a[...], ga1r[...].reshape(512, 512)).astype(BF).reshape(NU, 32, 512)
    grad_a2[0]()
    sent.append(grad_b1[1]())
    gb2[...] = mm(p_at[...], gb1r[...].reshape(512, 512)).astype(BF).reshape(NY, 64, 512)
    grad_b2[0]()
    rows2[0]()

    for i in (3, 4, 5):
        in_copies[i].wait()

    def step(got, own, recv, half, out, cross):
        sent.append(got())
        gradient = mm(own[...], recv[...].reshape(512, 512))
        for b in range(NX):
            at = pl.ds(2 * b + half, 128, stride=8)
            updated, first_new, second_new = adam_update(
                gradient[:, b * 128 : (b + 1) * 128], mas[at, :], one[at, :], two[at, :]
            )
            mas_n[at, :] = updated
            one_n[at, :] = first_new
            two_n[at, :] = second_new
            out[b] = updated.astype(BF)
        cross()

    step(grad_a2[1], own_a, ga2r, 0, wa, cross_a[0])
    step(grad_b2[1], own_b, gb2r, 1, wb, cross_b[0])
    outs = [(mas_n, mas_o), (one_n, one_o), (two_n, two_o)]
    out_copies = [pltpu.make_async_copy(s, d, out_sem.at[i]) for i, (s, d) in enumerate(outs)]
    for c in out_copies:
        c.start()

    def place_weights(got, x, table, out, start):
        sent.append(got())
        table[...] = mm(p_c[...], x[...].reshape(512, 128)).astype(BF).reshape(EXPERTS, 16, 128)

        @pl.loop(0, NY)
        def _(a):
            for b in range(NU):
                out[a, b] = table[new_s[a * NU + b]]

        start()

    place_weights(cross_a[1], xa, ya, oa1, weight_a1[0])
    place_weights(cross_b[1], xb, yb, ob1, weight_b1[0])

    sent.append(rows2[1]())
    rowsx[0]()
    sent.append(weight_a1[1]())
    weight_a2[0]()
    sent.append(weight_b1[1]())
    weight_b2[0]()
    sent.append(rowsx[1]())
    for b in range(4):
        lanes = jnp.concatenate(
            [rowx[m, :, :, b * 128 : (b + 1) * 128].reshape(256, 128) for m in range(NX)], axis=1
        )
        rowp[:, b * 512 : (b + 1) * 512] = mm(lanes, p_ct[...]).astype(BF)

    sent.append(weight_a2[1]())
    out_a = mm(rowp[...], wa2r[...].reshape(2048, 128)).astype(BF)
    ta1[...] = out_a.reshape(NU, 16, 128)
    back_a1[0]()
    sent.append(weight_b2[1]())
    out_b = mm(rowp[...], wb2r[...].reshape(2048, 128)).astype(BF)
    tb1[...] = mm(p_st[...], out_b).astype(BF).reshape(NY, 32, 128)
    back_b1[0]()
    sent.append(back_a1[1]())
    ta2[...] = mm(p_st[...], ta1r[...].reshape(256, 128)).astype(BF).reshape(NY, 32, 128)
    back_a2[0]()
    sent.append(back_b1[1]())
    tb2[...] = mm(p_s[...], tb1r[...].reshape(256, 128)).astype(BF).reshape(NU, 16, 128)
    back_b2[0]()

    def pick(s, got):
        return lax.dot_general(
            s[...], got[...].reshape(256, 128), (((0,), (0,)), ((), ())), preferred_element_type=F32
        ).astype(BF)

    sent.append(back_a2[1]())
    proj[:, :128] = pick(slots, ta2r)
    sent.append(back_b2[1]())
    proj[:, 128:] = pick(slots_u, tb2r)
    proj_copy = pltpu.make_async_copy(proj, proj_o, out_sem.at[3])
    proj_copy.start()
    for copy in sent:
        copy.wait_send()
    for c in out_copies:
        c.wait()
    proj_copy.wait()


def body(
    grad_cot, grad_hidden, old_place, master, moment_one, moment_two, new_place, rows, dest, counts
):
    state = jax.ShapeDtypeStruct((1024, 128), F32)
    hbm = pl.BlockSpec(memory_space=pl.ANY)
    vmem = pl.BlockSpec(memory_space=pltpu.VMEM)
    smem = pl.BlockSpec(memory_space=pltpu.SMEM)
    v = lambda *s: pltpu.VMEM(s, BF)
    f = lambda *s: pltpu.VMEM(s, F32)
    scratch = [
        v(1024, 512), v(1024, 1024), v(128, 512),
        f(1024, 128), f(1024, 128), f(1024, 128), f(1024, 128), f(1024, 128), f(1024, 128),
        v(128, 256),
        v(512, 512), v(512, 512), v(512, 512), v(512, 512), v(256, 256), v(256, 256),
        v(128, 512), v(128, 512), v(256, 128), v(256, 128),
        v(8, 32, 512), v(8, 32, 512), v(16, 16, 512), v(16, 16, 512), v(4, 16, 16, 512), v(256, 2048),
        v(8, 64, 512), v(8, 64, 512), v(16, 32, 512), v(16, 32, 512),
        v(512, 512), v(16, 32, 512), v(16, 32, 512), v(8, 64, 512), v(8, 64, 512),
        v(4, 128, 128), v(4, 128, 128), v(4, 128, 128), v(4, 128, 128), v(32, 16, 128), v(32, 16, 128),
        v(8, 16, 16, 128), v(8, 16, 16, 128), v(16, 8, 16, 128), v(8, 16, 16, 128),
        v(8, 16, 16, 128), v(8, 16, 16, 128),
        v(16, 16, 128), v(8, 32, 128), v(16, 16, 128), v(8, 32, 128),
        v(8, 32, 128), v(16, 16, 128), v(8, 32, 128), v(16, 16, 128),
        pltpu.SemaphoreType.DMA((6,)), pltpu.SemaphoreType.DMA((4,)), pltpu.SemaphoreType.DMA((17,)),
        pltpu.SemaphoreType.DMA((17,)), pltpu.SemaphoreType.DMA((17,)),
    ]
    updated, first_new, second_new, projected = pl.pallas_call(
        kernel,
        out_shape=(state, state, state, jax.ShapeDtypeStruct((128, 256), BF)),
        in_specs=[hbm, hbm, vmem, hbm, hbm, hbm, smem, hbm, vmem, smem],
        out_specs=(hbm, hbm, hbm, hbm),
        scratch_shapes=scratch,
        compiler_params=pltpu.CompilerParams(
            collective_id=0, has_side_effects=True, vmem_limit_bytes=48 * 1024 * 1024
        ),
        name="whole_step",
    )(
        grad_cot, grad_hidden, old_place.reshape(1, 128), master.reshape(1024, 128),
        moment_one.reshape(1024, 128), moment_two.reshape(1024, 128), new_place, rows,
        dest.reshape(1, 128), counts,
    )
    back = lambda a: a.reshape(EXPERTS, 1, 4096)
    return (back(updated), back(first_new), back(second_new), projected)


def solution(mesh):
    return jax.shard_map(
        body,
        mesh=mesh,
        in_specs=(
            P("dp", "mp"),
            P("dp", None),
            P(),
            P(None, "mp", "dp"),
            P(None, "mp", "dp"),
            P(None, "mp", "dp"),
            P(),
            P("dp", "mp"),
            P("dp"),
            P("dp"),
        ),
        out_specs=(P(None, "mp", "dp"), P(None, "mp", "dp"), P(None, "mp", "dp"), P("dp", "mp")),
        check_vma=False,
    )
```

time: 235 us -> 111 us (0.47)
  Pallas kernels: 0 us -> 99.1 us
  blocking collectives: 70.7 us -> 0 us
  waiting for transfers between devices: 62.9 us -> 0 us
  starting transfers between devices: 31.1 us -> 0 us
  local copies, waits for them, and re-layouts: 27 us -> 10.2 us
  other arithmetic: 15.4 us -> 0 us
  between operations: 14.8 us -> 1.31 us
  matrix products: 11.9 us -> 0 us
    pallas_call x0 -> x1, Pallas kernels: none -> 99.1 us  [body(): pl.pallas_call(kernel, out_shape=(state, state, state, jax.ShapeDtypeStru...]
    all_to_all x1 -> x0, blocking collectives: 70.7 us -> none  [body(): lax.all_to_all(pieces, 'dp', split_axis=0, concat_axis=0, tiled=True)]
    all_to_all x3 -> x0, waiting for transfers between devices: 34.2 us -> none  [the longest x1 27 us: body(): lax.all_to_all(outgoing, 'dp', split_axis=0, concat_axis=0, tiled=True)]
    all_to_all x3 -> x0, starting transfers between devices: 31 us -> none  [the longest x1 15.7 us: body(): lax.all_to_all(summed.astype(jnp.bfloat16), 'dp', split_axis=0, concat_ax...]
    reduce_scatter x1 -> x0, waiting for transfers between devices: 28.7 us -> none  [body(): lax.psum_scatter(partial_out, 'mp', scatter_dimension=2, tiled=True)]
    all_to_all x2 -> x0, other arithmetic: 12 us -> none  [body(): lax.all_to_all(outgoing, 'dp', split_axis=0, concat_axis=0, tiled=True)]
    dot_general x4 -> x0, matrix products: 11.9 us -> none  [the longest x1 3.85 us: body(): jnp.dot(owner_of, arrived, precision=lax.Precision.HIGHEST, preferred_ele...]
    unnamed x21 -> x20, local copies, waits for them, and re-layouts: 16.8 us -> 10.2 us
  transfers between devices with their start and end apart: 4 -> 0, of which waited for: 3 -> 0; matrix products, arithmetic and copies ran while one was open for 11% -> 0% of each run, Pallas kernels for 0% -> 0%
where the time goes in v1:
time: 111 us
  Pallas kernels  99.1 us (89%)
  local copies, waits for them, and re-layouts  10.2 us (9%)
  between operations  1.31 us (1%)
    pallas_call x1, Pallas kernels, body(): pl.pallas_call(kernel, out_shape=(state, state, state, jax.ShapeDtypeStru...  99.1 us
    unnamed x20, local copies, waits for them, and re-layouts  10.2 us

profile of v1, /device:TPU:1, one launch (start us, length us, event | category | flops | bytes accessed | tf_op | source)
XLA Modules:
  0.0 110.6 jit_solution(15809608569928763210)
XLA Ops:
  1.3 0.0 copy-start
  1.3 1.2 %copy-done = bf16[1024,512]{1,0:T(8,128)(2,1)S(1)} copy-done((bf16[1024,512]{1,0:T(8,128)(2,1)S(1)}, bf16[1024,512]{1,0:T(8,128)(2,1)}, u32[]{:S(2)}) %copy-start) | copy-done | bytes 1048600
  2.5 0.0 copy-start.1
  2.5 1.0 copy-done.1
  3.5 0.0 copy-start.2
  3.6 1.0 copy-done.2
  4.6 0.0 copy-start.3
  4.6 1.0 copy-done.3
  5.6 0.0 copy-start.4
  5.6 0.9 copy-done.4
  6.5 0.0 copy-start.5
  6.5 0.7 copy-done.5
  7.2 0.0 copy-start.6
  7.2 0.7 copy-done.6
  7.8 0.0 copy-start.7
  7.9 0.7 copy-done.7
  8.5 99.1 %whole_step.1 = (f32[1024,128]{1,0:T(8,128)S(1)}, f32[1024,128]{1,0:T(8,128)S(1)}, f32[1024,128]{1,0:T(8,128)S(1)}, bf16[128,256]{1,0:T(8,128)(2,1)S(1)}) custom-call(bf16[1024,512]{1,0:T(8,128)(2,1)S(1)} %copy-done, bf16[1024,1024]{1,0:T(8,128)(2,1)} %hid_h.1, s32[1,128]{1,0:T(1,128)S(1)} %bitcast.14, f32[1024,128]{1,0:T(8,128)S(1)} %bitcast.8, ...), custom_call_target="tpu_custom_call" | custom-call | tf_op jit(solution)/shard_map/whole_step/pallas_call | solution.py:332
  107.6 0.8 copy.22
  108.4 0.8 copy.23
  109.2 0.8 copy.24
  110.0 0.6 copy.25
Async XLA Ops:
  1.3 1.2 %copy-start = (bf16[1024,512]{1,0:T(8,128)(2,1)S(1)}, bf16[1024,512]{1,0:T(8,128)(2,1)}, u32[]{:S(2)}) copy-start(bf16[1024,512]{1,0:T(8,128)(2,1)} %cot_h.1) | copy-start | bytes 3145732
  2.5 1.0 copy-start.1
  3.5 1.0 copy-start.2
  4.6 1.0 copy-start.3
  5.6 0.9 copy-start.4
  6.5 0.7 copy-start.5
  7.2 0.7 copy-start.6
  7.8 0.7 copy-start.7

commit v2 on v1

--- a/solution.py
+++ b/solution.py
@@ -62,9 +62,10 @@
     mas_o, one_o, two_o, proj_o,
     cot, hid, rows, mas, one, two, mas_n, one_n, two_n, proj,
     p_a, p_at, p_c, p_ct, p_s, p_st, own_a, own_b, slots, slots_u,
-    row1, row1r, row2, row2r, rowx, rowp,
-    ga1, ga1r, ga2, ga2r, gb0, gb1, gb1r, gb2, gb2r,
-    wa, wb, xa, xb, ya, yb, oa1, ob1, wa1r, wb1r, wa2r, wb2r,
+    ra1, ra1r, ra2, ra2r, rb1, rb1r, rb2, rb2r, row, rowx, rowp,
+    ga0, ga0r, ga1, ga1r, ha, ha0, ha0r, ha1, ha1r,
+    gb0, gb0r, gb1, gb1r, hb, hb0, hb0r, hb1, hb1r,
+    wa, wb, xa, xb, ya, yb, oa, ob, da0, da1, db0, db1, wea, web,
     ta1, tb1, ta1r, tb1r, ta2, tb2, ta2r, tb2r,
     in_sem, out_sem, loc_sem, snd_sem, rcv_sem,
 ):
@@ -87,9 +88,14 @@
 
     rings = {"y": (NY, y, peer_y), "u": (NU, u, peer_u), "x": (NX, mp, peer_x)}
 
-    ins = [(cot_h, cot), (hid_h, hid), (rows_h, rows), (mas_h, mas), (one_h, one), (two_h, two)]
+    ins = [
+        (cot_h, cot), (rows_h, rows), (mas_h, mas), (one_h, one), (two_h, two),
+    ]
+    for b in range(NX):
+        at = pl.ds(b * 256, 256)
+        ins.append((hid_h.at[:, at], hid.at[:, at]))
     in_copies = [pltpu.make_async_copy(s, d, in_sem.at[i]) for i, (s, d) in enumerate(ins)]
-    for i in (2, 0, 1, 3, 4, 5):
+    for i in (1, 0, 5, 6, 7, 8, 2, 3, 4):
         in_copies[i].start()
 
     barrier = pltpu.get_barrier_semaphore()
@@ -140,24 +146,121 @@
         wait = lambda: finish(i, ring, src_all, dst_all, src, part, dst, place)
         return start, wait
 
-    rows1 = exchange(0, "y", row1, row1r)
-    rows2 = exchange(1, "u", row2, row2r)
-    rowsx = exchange(2, "x", row2r, rowx, part=whole_ref)
-    grad_a1 = exchange(3, "y", ga1, ga1r)
-    grad_a2 = exchange(4, "u", ga2, ga2r)
-    grad_b1 = exchange(5, "u", gb1, gb1r)
-    grad_b2 = exchange(6, "y", gb2, gb2r)
-    cross_a = exchange(7, "x", wa, xa)
-    cross_b = exchange(8, "x", wb, xb)
-    weight_a1 = exchange(9, "u", oa1, wa1r, part=second)
-    weight_a2 = exchange(10, "y", wa1r, wa2r, part=second)
-    weight_b1 = exchange(11, "y", ob1, wb1r)
-    weight_b2 = exchange(12, "u", wb1r, wb2r, part=second, place=second)
-    back_a1 = exchange(13, "u", ta1, ta1r)
-    back_a2 = exchange(14, "y", ta2, ta2r)
-    back_b1 = exchange(15, "y", tb1, tb1r)
-    back_b2 = exchange(16, "u", tb2, tb2r)
+    rows_a1 = exchange(0, "y", ra1, ra1r)
+    rows_a2 = exchange(1, "u", ra2, ra2r)
+    rows_b1 = exchange(2, "u", rb1, rb1r)
+    rows_b2 = exchange(3, "y", rb2, rb2r)
+    rowsx = exchange(4, "x", row, rowx, part=whole_ref)
+    grad_a = (exchange(5, "y", ga0, ga0r), exchange(6, "u", ga1, ga1r), exchange(7, "u", ha0, ha0r), exchange(8, "y", ha1, ha1r))
+    grad_b = (exchange(9, "y", gb0, gb0r), exchange(10, "u", gb1, gb1r), exchange(11, "u", hb0, hb0r), exchange(12, "y", hb1, hb1r))
+    cross_a = exchange(13, "x", wa, xa)
+    cross_b = exchange(14, "x", wb, xb)
+    back_a1 = exchange(15, "u", ta1, ta1r)
+    back_a2 = exchange(16, "y", ta2, ta2r)
+    back_b1 = exchange(17, "y", tb1, tb1r)
+    back_b2 = exchange(18, "u", tb2, tb2r)
     sent = []
+
+    z = u // 2
+    core = lax.rem(u, 2)
+
+    def remote(i, src, dst, device):
+        return pltpu.make_async_remote_copy(
+            src_ref=src, dst_ref=dst, send_sem=snd_sem.at[i], recv_sem=rcv_sem.at[i],
+            device_id=device, device_id_type=MESH,
+        )
+
+    def to_core(i, which, part, place):
+        def start():
+            @pl.loop(1, NU // 2)
+            def _(k):
+                t = lax.rem(z + k, NU // 2)
+                remote(i, part(t), place(u), (y * NU + t * 2 + which, mp)).start()
+
+            @pl.when(core == which)
+            def _():
+                pltpu.make_async_copy(part(z), place(u), loc_sem.at[i]).start()
+
+            @pl.when(core != which)
+            def _():
+                remote(i, part(z), place(u), (y * NU + z * 2 + which, mp)).start()
+
+        def wait(gap):
+            @pl.when(core == which)
+            def _():
+                pltpu.make_async_copy(part(z), place(u), loc_sem.at[i]).wait()
+                remote(i, gap(NU - 1), gap(NU - 1), peer_u(1)[1]).wait_recv()
+
+        def wait_send(gap):
+            @pl.when(core == which)
+            def _():
+                remote(i, gap(NU // 2 - 1), gap(NU // 2 - 1), peer_u(1)[1]).wait_send()
+
+            @pl.when(core != which)
+            def _():
+                remote(i, gap(NU // 2), gap(NU // 2), peer_u(1)[1]).wait_send()
+
+        return start, wait, wait_send
+
+    def along_y(i, part, place):
+        def start():
+            @pl.loop(1, NY)
+            def _(k):
+                t, device = peer_y(k)
+                remote(i, part(t), place(y), device).start()
+
+            pltpu.make_async_copy(part(y), place(y), loc_sem.at[i]).start()
+
+        def wait(gap):
+            pltpu.make_async_copy(part(y), place(y), loc_sem.at[i]).wait()
+            remote(i, gap(NY - 1), gap(NY - 1), peer_y(1)[1]).wait_recv()
+
+        def wait_send(gap):
+            remote(i, gap(NY - 1), gap(NY - 1), peer_y(1)[1]).wait_send()
+
+        return start, wait, wait_send
+
+    def weight_path(i, out, d0, d1, got):
+        first0 = to_core(i, 0, lambda t: out.at[:, t, 0], lambda s: d0.at[s])
+        first1 = along_y(i + 1, lambda t: out.at[t, :, 1], lambda s: d1.at[s])
+        then0 = along_y(i + 2, lambda t: d0.at[:, t], lambda s: got.at[s])
+        then1 = to_core(i + 3, 1, lambda t: d1.at[:, t], lambda s: got.at[:, s])
+
+        def first():
+            first0[0]()
+            first1[0]()
+
+        def then():
+            first0[1](lambda n: d0.at[pl.ds(0, n)])
+
+            @pl.when(core == 0)
+            def _():
+                then0[0]()
+
+            first1[1](lambda n: d1.at[pl.ds(0, n)])
+            then1[0]()
+
+        def last():
+            @pl.when(core == 0)
+            def _():
+                then0[1](lambda n: got.at[pl.ds(0, n)])
+
+            then1[1](lambda n: got.at[:, pl.ds(0, n)])
+
+        def sends():
+            first0[2](lambda n: d0.at[pl.ds(0, n)])
+            first1[2](lambda n: d1.at[pl.ds(0, n)])
+
+            @pl.when(core == 0)
+            def _():
+                then0[2](lambda n: got.at[pl.ds(0, n)])
+
+            then1[2](lambda n: got.at[:, pl.ds(0, n)])
+
+        return first, then, last, sends
+
+    weight_a = weight_path(19, oa, da0, da1, wea)
+    weight_b = weight_path(23, ob, db0, db1, web)
 
     dest = jnp.broadcast_to(dest_ref[...], (128, 128))
     dest_t = dest.astype(F32).T.astype(I32)
@@ -169,30 +272,39 @@
     slot_u = jnp.where(live, (dest_row & 15) * 16 + (dest_row >> 4) * 2 + rank, -1)
     slots[...] = ones_where(iota((256, 128), 0) == jnp.broadcast_to(slot_y, (256, 128)))
     slots_u[...] = ones_where(iota((256, 128), 0) == jnp.broadcast_to(slot_u, (256, 128)))
-    in_copies[2].wait()
-    row1[...] = mm(slots[...], rows[...]).astype(BF).reshape(NY, 32, 512)
-
+    in_copies[1].wait()
+    ra1[...] = mm(slots[...], rows[:, :256]).astype(BF).reshape(NY, 32, 256)
+    rb1[...] = mm(slots_u[...], rows[:, 256:]).astype(BF).reshape(NU, 16, 256)
+
+    pl.semaphore_wait(barrier, NY - 1 + NU - 1 + NX - 1)
+    rows_a1[0]()
+    rows_b1[0]()
     p_a[...] = reorder(3, 4, 2)
 
-    pl.semaphore_wait(barrier, NY - 1 + NU - 1 + NX - 1)
-    rows1[0]()
-
     in_copies[0].wait()
-    in_copies[1].wait()
-
-    @pl.loop(0, NX)
-    def _(b):
-        at = pl.multiple_of(b * 256, 256)
-        to = pl.multiple_of(b * 128, 128)
-        part = lax.dot_general(
-            cot[...], hid[:, pl.ds(at, 256)], (((0,), (0,)), ((), ())), preferred_element_type=F32
+
+    def partial(b):
+        in_copies[5 + b].wait()
+        return lax.dot_general(
+            cot[...], hid[:, b * 256 : (b + 1) * 256], (((0,), (0,)), ((), ())), preferred_element_type=F32
         ).astype(BF)
-        ga1[:, :, pl.ds(to, 128)] = part[:, :128].reshape(NY, 64, 128)
-        gb0[:, pl.ds(to, 128)] = part[:, 128:]
-
-    grad_a1[0]()
-    gb1[...] = mm(p_a[...], gb0[...]).astype(BF).reshape(NU, 32, 512)
-    grad_b1[0]()
+
+    for b in range(2):
+        lanes = slice(b * 128, (b + 1) * 128)
+        part = partial(b)
+        ga0[:, :, lanes] = part[:, :128].reshape(NY, 64, 128)
+        gb0[:, :, lanes] = part[:, 128:].reshape(NY, 64, 128)
+    grad_a[0][0]()
+    for b in range(2):
+        lanes = slice(b * 128, (b + 1) * 128)
+        part = partial(2 + b)
+        ha[:, lanes] = part[:, :128]
+        hb[:, lanes] = part[:, 128:]
+    ha0[...] = mm(p_a[...], ha[...]).astype(BF).reshape(NU, 32, 256)
+    grad_a[2][0]()
+    grad_b[0][0]()
+    hb0[...] = mm(p_a[...], hb[...]).astype(BF).reshape(NU, 32, 256)
+    grad_b[2][0]()
 
     p_at[...] = reorder(4, 3, 2)
     p_s[...] = reorder(3, 4, 1)
@@ -208,40 +320,41 @@
         wanted = holder * 4 + (iota((1, 512), 1) & 3)
         own[...] = ones_where(iota((128, 512), 0) == jnp.broadcast_to(wanted, (128, 512)))
 
-    sent.append(rows1[1]())
-    row2[...] = mm(p_s[...], row1r[...].reshape(256, 512)).astype(BF).reshape(NU, 16, 512)
-
-    sent.append(grad_a1[1]())
-    ga2[...] = mm(p_a[...], ga1r[...].reshape(512, 512)).astype(BF).reshape(NU, 32, 512)
-    grad_a2[0]()
-    sent.append(grad_b1[1]())
-    gb2[...] = mm(p_at[...], gb1r[...].reshape(512, 512)).astype(BF).reshape(NY, 64, 512)
-    grad_b2[0]()
-    rows2[0]()
-
-    for i in (3, 4, 5):
+    sent.append(rows_a1[1]())
+    ra2[...] = mm(p_s[...], ra1r[...].reshape(256, 256)).astype(BF).reshape(NU, 16, 256)
+    sent.append(rows_b1[1]())
+    rb2[...] = mm(p_st[...], rb1r[...].reshape(256, 256)).astype(BF).reshape(NY, 32, 256)
+
+    def turn(grad, g0r, g1, h0r, h1):
+        sent.append(grad[0][1]())
+        g1[...] = mm(p_a[...], g0r[...].reshape(512, 256)).astype(BF).reshape(NU, 32, 256)
+        grad[1][0]()
+        sent.append(grad[2][1]())
+        h1[...] = mm(p_at[...], h0r[...].reshape(512, 256)).astype(BF).reshape(NY, 64, 256)
+        grad[3][0]()
+
+    turn(grad_a, ga0r, ga1, ha0r, ha1)
+    turn(grad_b, gb0r, gb1, hb0r, hb1)
+    rows_a2[0]()
+    rows_b2[0]()
+
+    for i in (2, 3, 4):
         in_copies[i].wait()
 
-    def step(got, own, recv, half, out, cross):
-        sent.append(got())
-        gradient = mm(own[...], recv[...].reshape(512, 512))
-        for b in range(NX):
-            at = pl.ds(2 * b + half, 128, stride=8)
-            updated, first_new, second_new = adam_update(
-                gradient[:, b * 128 : (b + 1) * 128], mas[at, :], one[at, :], two[at, :]
-            )
-            mas_n[at, :] = updated
-            one_n[at, :] = first_new
-            two_n[at, :] = second_new
-            out[b] = updated.astype(BF)
+    def step(grad, g1r, h1r, half, out, cross):
+        for pair, own, recv, got in ((0, own_a, g1r, grad[1][1]), (2, own_b, h1r, grad[3][1])):
+            sent.append(got())
+            gradient = mm(own[...], recv[...].reshape(512, 256))
+            for b in range(2):
+                at = pl.ds(2 * (pair + b) + half, 128, stride=8)
+                updated, first_new, second_new = adam_update(
+                    gradient[:, b * 128 : (b + 1) * 128], mas[at, :], one[at, :], two[at, :]
+                )
+                mas_n[at, :] = updated
+                one_n[at, :] = first_new
+                two_n[at, :] = second_new
+                out[pair + b] = updated.astype(BF)
         cross()
-
-    step(grad_a2[1], own_a, ga2r, 0, wa, cross_a[0])
-    step(grad_b2[1], own_b, gb2r, 1, wb, cross_b[0])
-    outs = [(mas_n, mas_o), (one_n, one_o), (two_n, two_o)]
-    out_copies = [pltpu.make_async_copy(s, d, out_sem.at[i]) for i, (s, d) in enumerate(outs)]
-    for c in out_copies:
-        c.start()
 
     def place_weights(got, x, table, out, start):
         sent.append(got())
@@ -250,19 +363,27 @@
         @pl.loop(0, NY)
         def _(a):
             for b in range(NU):
-                out[a, b] = table[new_s[a * NU + b]]
+                out[a, b // 2, b % 2] = table[new_s[a * NU + b]]
 
         start()
 
-    place_weights(cross_a[1], xa, ya, oa1, weight_a1[0])
-    place_weights(cross_b[1], xb, yb, ob1, weight_b1[0])
-
-    sent.append(rows2[1]())
+    step(grad_a, ga1r, ha1r, 0, wa, cross_a[0])
+    place_weights(cross_a[1], xa, ya, oa, weight_a[0])
+    step(grad_b, gb1r, hb1r, 1, wb, cross_b[0])
+    outs = [(mas_n, mas_o), (one_n, one_o), (two_n, two_o), (proj, proj_o)]
+    out_copies = [pltpu.make_async_copy(s, d, out_sem.at[i]) for i, (s, d) in enumerate(outs)]
+    for c in out_copies[:3]:
+        c.start()
+
+    place_weights(cross_b[1], xb, yb, ob, weight_b[0])
+
+    sent.append(rows_a2[1]())
+    row[:, :, :256] = ra2r[...]
+    sent.append(rows_b2[1]())
+    row[:, :, 256:] = mm(p_s[...], rb2r[...].reshape(256, 256)).astype(BF).reshape(NU, 16, 256)
     rowsx[0]()
-    sent.append(weight_a1[1]())
-    weight_a2[0]()
-    sent.append(weight_b1[1]())
-    weight_b2[0]()
+    weight_a[1]()
+    weight_b[1]()
     sent.append(rowsx[1]())
     for b in range(4):
         lanes = jnp.concatenate(
@@ -270,12 +391,12 @@
         )
         rowp[:, b * 512 : (b + 1) * 512] = mm(lanes, p_ct[...]).astype(BF)
 
-    sent.append(weight_a2[1]())
-    out_a = mm(rowp[...], wa2r[...].reshape(2048, 128)).astype(BF)
+    weight_a[2]()
+    out_a = mm(rowp[...], wea[...].reshape(2048, 128)).astype(BF)
     ta1[...] = out_a.reshape(NU, 16, 128)
     back_a1[0]()
-    sent.append(weight_b2[1]())
-    out_b = mm(rowp[...], wb2r[...].reshape(2048, 128)).astype(BF)
+    weight_b[2]()
+    out_b = mm(rowp[...], web[...].reshape(2048, 128)).astype(BF)
     tb1[...] = mm(p_st[...], out_b).astype(BF).reshape(NY, 32, 128)
     back_b1[0]()
     sent.append(back_a1[1]())
@@ -294,20 +415,33 @@
     proj[:, :128] = pick(slots, ta2r)
     sent.append(back_b2[1]())
     proj[:, 128:] = pick(slots_u, tb2r)
-    proj_copy = pltpu.make_async_copy(proj, proj_o, out_sem.at[3])
-    proj_copy.start()
+    out_copies[3].start()
     for copy in sent:
         copy.wait_send()
+    weight_a[3]()
+    weight_b[3]()
     for c in out_copies:
         c.wait()
-    proj_copy.wait()
+
+
+def commit(a, b, c, d, a_o, b_o, c_o, d_o, a_v, b_v, c_v, d_v, sem):
+    moves = ((d, d_v, d_o), (a, a_v, a_o), (b, b_v, b_o), (c, c_v, c_o))
+    gets = [pltpu.make_async_copy(x, v, sem.at[i]) for i, (x, v, _) in enumerate(moves)]
+    puts = [pltpu.make_async_copy(v, o, sem.at[4 + i]) for i, (_, v, o) in enumerate(moves)]
+    for get in gets:
+        get.start()
+    for get, put in zip(gets, puts):
+        get.wait()
+        put.start()
+    for put in puts:
+        put.wait()
 
 
 def body(
     grad_cot, grad_hidden, old_place, master, moment_one, moment_two, new_place, rows, dest, counts
 ):
     state = jax.ShapeDtypeStruct((1024, 128), F32)
-    hbm = pl.BlockSpec(memory_space=pl.ANY)
+    hbm = pl.BlockSpec(memory_space=pltpu.HBM)
     vmem = pl.BlockSpec(memory_space=pltpu.VMEM)
     smem = pl.BlockSpec(memory_space=pltpu.SMEM)
     v = lambda *s: pltpu.VMEM(s, BF)
@@ -318,25 +452,31 @@
         v(128, 256),
         v(512, 512), v(512, 512), v(512, 512), v(512, 512), v(256, 256), v(256, 256),
         v(128, 512), v(128, 512), v(256, 128), v(256, 128),
-        v(8, 32, 512), v(8, 32, 512), v(16, 16, 512), v(16, 16, 512), v(4, 16, 16, 512), v(256, 2048),
-        v(8, 64, 512), v(8, 64, 512), v(16, 32, 512), v(16, 32, 512),
-        v(512, 512), v(16, 32, 512), v(16, 32, 512), v(8, 64, 512), v(8, 64, 512),
+        v(8, 32, 256), v(8, 32, 256), v(16, 16, 256), v(16, 16, 256),
+        v(16, 16, 256), v(16, 16, 256), v(8, 32, 256), v(8, 32, 256),
+        v(16, 16, 512), v(4, 16, 16, 512), v(256, 2048),
+        v(8, 64, 256), v(8, 64, 256), v(16, 32, 256), v(16, 32, 256),
+        v(512, 256), v(16, 32, 256), v(16, 32, 256), v(8, 64, 256), v(8, 64, 256),
+        v(8, 64, 256), v(8, 64, 256), v(16, 32, 256), v(16, 32, 256),
+        v(512, 256), v(16, 32, 256), v(16, 32, 256), v(8, 64, 256), v(8, 64, 256),
         v(4, 128, 128), v(4, 128, 128), v(4, 128, 128), v(4, 128, 128), v(32, 16, 128), v(32, 16, 128),
-        v(8, 16, 16, 128), v(8, 16, 16, 128), v(16, 8, 16, 128), v(8, 16, 16, 128),
+        v(8, 8, 2, 16, 128), v(8, 8, 2, 16, 128),
+        v(16, 8, 16, 128), v(8, 8, 16, 128), v(16, 8, 16, 128), v(8, 8, 16, 128),
         v(8, 16, 16, 128), v(8, 16, 16, 128),
         v(16, 16, 128), v(8, 32, 128), v(16, 16, 128), v(8, 32, 128),
         v(8, 32, 128), v(16, 16, 128), v(8, 32, 128), v(16, 16, 128),
-        pltpu.SemaphoreType.DMA((6,)), pltpu.SemaphoreType.DMA((4,)), pltpu.SemaphoreType.DMA((17,)),
-        pltpu.SemaphoreType.DMA((17,)), pltpu.SemaphoreType.DMA((17,)),
+        pltpu.SemaphoreType.DMA((9,)), pltpu.SemaphoreType.DMA((4,)), pltpu.SemaphoreType.DMA((27,)),
+        pltpu.SemaphoreType.DMA((27,)), pltpu.SemaphoreType.DMA((27,)),
     ]
-    updated, first_new, second_new, projected = pl.pallas_call(
+    shapes = (state, state, state, jax.ShapeDtypeStruct((128, 256), BF))
+    results = pl.pallas_call(
         kernel,
-        out_shape=(state, state, state, jax.ShapeDtypeStruct((128, 256), BF)),
+        out_shape=shapes,
         in_specs=[hbm, hbm, vmem, hbm, hbm, hbm, smem, hbm, vmem, smem],
-        out_specs=(hbm, hbm, hbm, hbm),
+        out_specs=(hbm,) * 4,
         scratch_shapes=scratch,
         compiler_params=pltpu.CompilerParams(
-            collective_id=0, has_side_effects=True, vmem_limit_bytes=48 * 1024 * 1024
+            collective_id=0, has_side_effects=True, vmem_limit_bytes=67043328
         ),
         name="whole_step",
     )(
@@ -344,6 +484,15 @@
         moment_one.reshape(1024, 128), moment_two.reshape(1024, 128), new_place, rows,
         dest.reshape(1, 128), counts,
     )
+    updated, first_new, second_new, projected = pl.pallas_call(
+        commit,
+        out_shape=shapes,
+        in_specs=[hbm] * 4,
+        out_specs=(hbm,) * 4,
+        scratch_shapes=[f(1024, 128), f(1024, 128), f(1024, 128), v(128, 256), pltpu.SemaphoreType.DMA((8,))],
+        compiler_params=pltpu.CompilerParams(vmem_limit_bytes=67043328),
+        name="commit",
+    )(*results)
     back = lambda a: a.reshape(EXPERTS, 1, 4096)
     return (back(updated), back(first_new), back(second_new), projected)
 

time: 111 us -> 89.5 us (0.81)
  Pallas kernels: 99.1 us -> 88.1 us
  local copies, waits for them, and re-layouts: 10.2 us -> 0 us
    pallas_call x1 -> x2, Pallas kernels: 99.1 us -> 88.1 us  [the longest x1 85.8 us: body(): pl.pallas_call(kernel, out_shape=shapes, in_specs=[hbm, hbm, vmem, hbm, h...]
    unnamed x20 -> x0, local copies, waits for them, and re-layouts: 10.2 us -> none
where the time goes in v2:
time: 89.5 us; the launch traced here: 89.4 us
  Pallas kernels  88.1 us (98%)
  between operations  1.29 us (1%)
    pallas_call x1, Pallas kernels, body(): pl.pallas_call(kernel, out_shape=shapes, in_specs=[hbm, hbm, vmem, hbm, h...  85.8 us
    pallas_call x1, Pallas kernels, body(): pl.pallas_call(commit, out_shape=shapes, in_specs=[hbm] * 4, out_specs=(h...  2.29 us

profile of v2, /device:TPU:1, one launch (start us, length us, event | category | flops | bytes accessed | tf_op | source)
XLA Modules:
  0.0 89.4 jit_solution(17628648434616686366)
XLA Ops:
  1.3 85.8 %whole_step.1 = (f32[1024,128]{1,0:T(8,128)}, f32[1024,128]{1,0:T(8,128)}, f32[1024,128]{1,0:T(8,128)}, bf16[128,256]{1,0:T(8,128)(2,1)}) custom-call(bf16[1024,512]{1,0:T(8,128)(2,1)} %cot_h.1, bf16[1024,1024]{1,0:T(8,128)(2,1)} %hid_h.1, s32[1,128]{1,0:T(1,128)} %bitcast.11, f32[1024,128]{1,0:T(8,128)} %bitcast.8, f32[1024,128]{1,0:T(8,128)} %bitcast.9, ...), custom_call_target="tpu_custom_call" | custom-call | tf_op jit(solution)/shard_map/whole_step/pallas_call | solution.py:472
  87.1 2.3 %commit.1 = (f32[1024,128]{1,0:T(8,128)}, f32[1024,128]{1,0:T(8,128)}, f32[1024,128]{1,0:T(8,128)}, bf16[128,256]{1,0:T(8,128)(2,1)}) custom-call(f32[1024,128]{1,0:T(8,128)} %get-tuple-element.12.a, f32[1024,128]{1,0:T(8,128)} %get-tuple-element.13.b, f32[1024,128]{1,0:T(8,128)} %get-tuple-element.14.c, bf16[128,256]{1,0:T(8,128)(2,1)} %get-tuple-element.15.d), custom_call_target="tpu_custom_call" | custom-call | tf_op jit(solution)/shard_map/commit/pallas_call | solution.py:487

commit v3 on v2

--- a/solution.py
+++ b/solution.py
@@ -58,16 +58,16 @@
 
 
 def kernel(
-    cot_h, hid_h, old_ref, mas_h, one_h, two_h, new_s, rows_h, dest_ref, counts_s,
-    mas_o, one_o, two_o, proj_o,
-    cot, hid, rows, mas, one, two, mas_n, one_n, two_n, proj,
+    cot_h, hid_h, old_h, mas_h, one_h, two_h, new_s, rows_h, dest_h, counts_s,
+    mas_n, one_n, two_n, proj,
+    cot, cot_t, hid, rows, mas, one, two, old_ref, dest_ref,
     p_a, p_at, p_c, p_ct, p_s, p_st, own_a, own_b, slots, slots_u,
-    ra1, ra1r, ra2, ra2r, rb1, rb1r, rb2, rb2r, row, rowx, rowp,
+    ra1, ra1r, ra2, ra2r, rb1, rb1r, rb2, rb2r, row, rowx, rowp, rowq,
     ga0, ga0r, ga1, ga1r, ha, ha0, ha0r, ha1, ha1r,
     gb0, gb0r, gb1, gb1r, hb, hb0, hb0r, hb1, hb1r,
     wa, wb, xa, xb, ya, yb, oa, ob, da0, da1, db0, db1, wea, web,
     ta1, tb1, ta1r, tb1r, ta2, tb2, ta2r, tb2r,
-    in_sem, out_sem, loc_sem, snd_sem, rcv_sem,
+    in_sem, loc_sem, snd_sem, rcv_sem,
 ):
     me = lax.axis_index("dp")
     mp = lax.axis_index("mp")
@@ -85,6 +85,9 @@
     def peer_x(k):
         t = lax.rem(mp + k, NX)
         return t, (me, t)
+
+    def hop(k, n):
+        return n // 2 + lax.rem(k + 1, 2) * (k // 2) - lax.rem(k, 2) * (k // 2)
 
     rings = {"y": (NY, y, peer_y), "u": (NU, u, peer_u), "x": (NX, mp, peer_x)}
 
@@ -94,8 +97,9 @@
     for b in range(NX):
         at = pl.ds(b * 256, 256)
         ins.append((hid_h.at[:, at], hid.at[:, at]))
+    ins += [(dest_h, dest_ref), (old_h, old_ref)]
     in_copies = [pltpu.make_async_copy(s, d, in_sem.at[i]) for i, (s, d) in enumerate(ins)]
-    for i in (1, 0, 5, 6, 7, 8, 2, 3, 4):
+    for i in (9, 1, 0, 5, 6, 7, 8, 10, 2, 3, 4):
         in_copies[i].start()
 
     barrier = pltpu.get_barrier_semaphore()
@@ -111,7 +115,7 @@
         def start():
             @pl.loop(1, n)
             def _(k):
-                t, device = peer(k)
+                t, device = peer(hop(k, n))
                 pltpu.make_async_remote_copy(
                     src_ref=part(src, t), dst_ref=place(dst, mine), send_sem=snd_sem.at[i],
                     recv_sem=rcv_sem.at[i], device_id=device, device_id_type=MESH,
@@ -174,7 +178,7 @@
         def start():
             @pl.loop(1, NU // 2)
             def _(k):
-                t = lax.rem(z + k, NU // 2)
+                t = lax.rem(z + hop(k, NU // 2), NU // 2)
                 remote(i, part(t), place(u), (y * NU + t * 2 + which, mp)).start()
 
             @pl.when(core == which)
@@ -206,7 +210,7 @@
         def start():
             @pl.loop(1, NY)
             def _(k):
-                t, device = peer_y(k)
+                t, device = peer_y(hop(k, NY))
                 remote(i, part(t), place(y), device).start()
 
             pltpu.make_async_copy(part(y), place(y), loc_sem.at[i]).start()
@@ -261,6 +265,8 @@
 
     weight_a = weight_path(19, oa, da0, da1, wea)
     weight_b = weight_path(23, ob, db0, db1, web)
+
+    in_copies[9].wait()
 
     dest = jnp.broadcast_to(dest_ref[...], (128, 128))
     dest_t = dest.astype(F32).T.astype(I32)
@@ -282,12 +288,11 @@
     p_a[...] = reorder(3, 4, 2)
 
     in_copies[0].wait()
+    cot_t[...] = cot[...].T
 
     def partial(b):
         in_copies[5 + b].wait()
-        return lax.dot_general(
-            cot[...], hid[:, b * 256 : (b + 1) * 256], (((0,), (0,)), ((), ())), preferred_element_type=F32
-        ).astype(BF)
+        return mm(cot_t[...], hid[:, b * 256 : (b + 1) * 256]).astype(BF)
 
     for b in range(2):
         lanes = slice(b * 128, (b + 1) * 128)
@@ -311,6 +316,7 @@
     p_st[...] = reorder(4, 3, 1)
     p_c[...] = reorder(2, 5, 2)
     p_ct[...] = reorder(5, 2, 2)
+    in_copies[10].wait()
     old = jnp.broadcast_to(old_ref[...], (8, 128)).astype(F32).astype(BF)
     spread_b = ones_where(iota((128, 512), 0) == (iota((128, 512), 1) >> 2))
     col = iota((128, 512), 1)
@@ -370,11 +376,6 @@
     step(grad_a, ga1r, ha1r, 0, wa, cross_a[0])
     place_weights(cross_a[1], xa, ya, oa, weight_a[0])
     step(grad_b, gb1r, hb1r, 1, wb, cross_b[0])
-    outs = [(mas_n, mas_o), (one_n, one_o), (two_n, two_o), (proj, proj_o)]
-    out_copies = [pltpu.make_async_copy(s, d, out_sem.at[i]) for i, (s, d) in enumerate(outs)]
-    for c in out_copies[:3]:
-        c.start()
-
     place_weights(cross_b[1], xb, yb, ob, weight_b[0])
 
     sent.append(rows_a2[1]())
@@ -389,15 +390,17 @@
         lanes = jnp.concatenate(
             [rowx[m, :, :, b * 128 : (b + 1) * 128].reshape(256, 128) for m in range(NX)], axis=1
         )
-        rowp[:, b * 512 : (b + 1) * 512] = mm(lanes, p_ct[...]).astype(BF)
+        turned = mm(lanes, p_ct[...]).astype(BF)
+        rowp[:, b * 512 : (b + 1) * 512] = turned
+        rowq[:, b * 512 : (b + 1) * 512] = mm(p_st[...], turned).astype(BF)
 
     weight_a[2]()
     out_a = mm(rowp[...], wea[...].reshape(2048, 128)).astype(BF)
     ta1[...] = out_a.reshape(NU, 16, 128)
     back_a1[0]()
     weight_b[2]()
-    out_b = mm(rowp[...], web[...].reshape(2048, 128)).astype(BF)
-    tb1[...] = mm(p_st[...], out_b).astype(BF).reshape(NY, 32, 128)
+    out_b = mm(rowq[...], web[...].reshape(2048, 128)).astype(BF)
+    tb1[...] = out_b.reshape(NY, 32, 128)
     back_b1[0]()
     sent.append(back_a1[1]())
     ta2[...] = mm(p_st[...], ta1r[...].reshape(256, 128)).astype(BF).reshape(NY, 32, 128)
@@ -415,23 +418,16 @@
     proj[:, :128] = pick(slots, ta2r)
     sent.append(back_b2[1]())
     proj[:, 128:] = pick(slots_u, tb2r)
-    out_copies[3].start()
     for copy in sent:
         copy.wait_send()
     weight_a[3]()
     weight_b[3]()
-    for c in out_copies:
-        c.wait()
-
-
-def commit(a, b, c, d, a_o, b_o, c_o, d_o, a_v, b_v, c_v, d_v, sem):
-    moves = ((d, d_v, d_o), (a, a_v, a_o), (b, b_v, b_o), (c, c_v, c_o))
-    gets = [pltpu.make_async_copy(x, v, sem.at[i]) for i, (x, v, _) in enumerate(moves)]
-    puts = [pltpu.make_async_copy(v, o, sem.at[4 + i]) for i, (_, v, o) in enumerate(moves)]
-    for get in gets:
-        get.start()
-    for get, put in zip(gets, puts):
-        get.wait()
+
+
+def commit(a, b, c, d, a_o, b_o, c_o, d_o, sem):
+    moves = ((a, a_o), (b, b_o), (c, c_o), (d, d_o))
+    puts = [pltpu.make_async_copy(v, o, sem.at[i]) for i, (v, o) in enumerate(moves)]
+    for put in puts:
         put.start()
     for put in puts:
         put.wait()
@@ -444,17 +440,17 @@
     hbm = pl.BlockSpec(memory_space=pltpu.HBM)
     vmem = pl.BlockSpec(memory_space=pltpu.VMEM)
     smem = pl.BlockSpec(memory_space=pltpu.SMEM)
+    pin = lambda x: pltpu.with_memory_space_constraint(x, pltpu.HBM)
     v = lambda *s: pltpu.VMEM(s, BF)
     f = lambda *s: pltpu.VMEM(s, F32)
     scratch = [
-        v(1024, 512), v(1024, 1024), v(128, 512),
-        f(1024, 128), f(1024, 128), f(1024, 128), f(1024, 128), f(1024, 128), f(1024, 128),
-        v(128, 256),
+        v(1024, 512), v(512, 1024), v(1024, 1024), v(128, 512),
+        f(1024, 128), f(1024, 128), f(1024, 128), pltpu.VMEM((1, 128), I32), pltpu.VMEM((1, 128), I32),
         v(512, 512), v(512, 512), v(512, 512), v(512, 512), v(256, 256), v(256, 256),
         v(128, 512), v(128, 512), v(256, 128), v(256, 128),
         v(8, 32, 256), v(8, 32, 256), v(16, 16, 256), v(16, 16, 256),
         v(16, 16, 256), v(16, 16, 256), v(8, 32, 256), v(8, 32, 256),
-        v(16, 16, 512), v(4, 16, 16, 512), v(256, 2048),
+        v(16, 16, 512), v(4, 16, 16, 512), v(256, 2048), v(256, 2048),
         v(8, 64, 256), v(8, 64, 256), v(16, 32, 256), v(16, 32, 256),
         v(512, 256), v(16, 32, 256), v(16, 32, 256), v(8, 64, 256), v(8, 64, 256),
         v(8, 64, 256), v(8, 64, 256), v(16, 32, 256), v(16, 32, 256),
@@ -465,32 +461,32 @@
         v(8, 16, 16, 128), v(8, 16, 16, 128),
         v(16, 16, 128), v(8, 32, 128), v(16, 16, 128), v(8, 32, 128),
         v(8, 32, 128), v(16, 16, 128), v(8, 32, 128), v(16, 16, 128),
-        pltpu.SemaphoreType.DMA((9,)), pltpu.SemaphoreType.DMA((4,)), pltpu.SemaphoreType.DMA((27,)),
+        pltpu.SemaphoreType.DMA((11,)), pltpu.SemaphoreType.DMA((27,)),
         pltpu.SemaphoreType.DMA((27,)), pltpu.SemaphoreType.DMA((27,)),
     ]
     shapes = (state, state, state, jax.ShapeDtypeStruct((128, 256), BF))
     results = pl.pallas_call(
         kernel,
         out_shape=shapes,
-        in_specs=[hbm, hbm, vmem, hbm, hbm, hbm, smem, hbm, vmem, smem],
-        out_specs=(hbm,) * 4,
+        in_specs=[hbm, hbm, hbm, hbm, hbm, hbm, smem, hbm, hbm, smem],
+        out_specs=(vmem,) * 4,
         scratch_shapes=scratch,
         compiler_params=pltpu.CompilerParams(
-            collective_id=0, has_side_effects=True, vmem_limit_bytes=67043328
+            collective_id=0, has_side_effects=True, vmem_limit_bytes=50331648
         ),
         name="whole_step",
     )(
-        grad_cot, grad_hidden, old_place.reshape(1, 128), master.reshape(1024, 128),
-        moment_one.reshape(1024, 128), moment_two.reshape(1024, 128), new_place, rows,
-        dest.reshape(1, 128), counts,
+        pin(grad_cot), pin(grad_hidden), pin(old_place.reshape(1, 128)), pin(master.reshape(1024, 128)),
+        pin(moment_one.reshape(1024, 128)), pin(moment_two.reshape(1024, 128)), pin(new_place), pin(rows),
+        pin(dest.reshape(1, 128)), counts,
     )
     updated, first_new, second_new, projected = pl.pallas_call(
         commit,
         out_shape=shapes,
-        in_specs=[hbm] * 4,
+        in_specs=[vmem] * 4,
         out_specs=(hbm,) * 4,
-        scratch_shapes=[f(1024, 128), f(1024, 128), f(1024, 128), v(128, 256), pltpu.SemaphoreType.DMA((8,))],
-        compiler_params=pltpu.CompilerParams(vmem_limit_bytes=67043328),
+        scratch_shapes=[pltpu.SemaphoreType.DMA((4,))],
+        compiler_params=pltpu.CompilerParams(vmem_limit_bytes=1048576),
         name="commit",
     )(*results)
     back = lambda a: a.reshape(EXPERTS, 1, 4096)

time: 89.5 us -> 83.7 us (0.935)
  Pallas kernels: 88.1 us -> 82.3 us
    pallas_call x2, Pallas kernels: 88.1 us -> 82.3 us  [the longest x1 81.1 us: body(): pl.pallas_call(kernel, out_shape=shapes, in_specs=[hbm, hbm, hbm, hbm, hb...]
where the time goes in v3:
time: 83.7 us; the launch traced here: 83.6 us
  Pallas kernels  82.3 us (98%)
  between operations  1.29 us (2%)
    pallas_call x1, Pallas kernels, body(): pl.pallas_call(kernel, out_shape=shapes, in_specs=[hbm, hbm, hbm, hbm, hb...  81.1 us

profile of v3, /device:TPU:1, one launch (start us, length us, event | category | flops | bytes accessed | tf_op | source)
XLA Modules:
  0.0 83.6 jit_solution(16297906579365814036)
XLA Ops:
  1.3 81.1 %whole_step.1 = (f32[1024,128]{1,0:T(8,128)S(1)}, f32[1024,128]{1,0:T(8,128)S(1)}, f32[1024,128]{1,0:T(8,128)S(1)}, bf16[128,256]{1,0:T(8,128)(2,1)S(1)}) custom-call(bf16[1024,512]{1,0:T(8,128)(2,1)} %cot_h.1, bf16[1024,1024]{1,0:T(8,128)(2,1)} %hid_h.1, s32[1,128]{1,0:T(1,128)} %bitcast.11, f32[1024,128]{1,0:T(8,128)} %bitcast.8, f32[1024,128]{1,0:T(8,128)} %bitcast.9, ...), custom_call_target="tpu_custom_call" | custom-call | tf_op jit(solution)/shard_map/whole_step/pallas_call | solution.py:468
  82.4 1.2 %commit.1 = (f32[1024,128]{1,0:T(8,128)}, f32[1024,128]{1,0:T(8,128)}, f32[1024,128]{1,0:T(8,128)}, bf16[128,256]{1,0:T(8,128)(2,1)}) custom-call(f32[1024,128]{1,0:T(8,128)S(1)} %get-tuple-element.12.a, f32[1024,128]{1,0:T(8,128)S(1)} %get-tuple-element.13.b, f32[1024,128]{1,0:T(8,128)S(1)} %get-tuple-element.14.c, bf16[128,256]{1,0:T(8,128)(2,1)S(1)} %get-tuple-element.15.d), custom_call_target="tpu_custom_call" | custom-call | tf_op jit(solution)/shard_map/commit/pallas_call | solution.py:483

commit v4 on v3

--- a/solution.py
+++ b/solution.py
@@ -60,7 +60,7 @@
 def kernel(
     cot_h, hid_h, old_h, mas_h, one_h, two_h, new_s, rows_h, dest_h, counts_s,
     mas_n, one_n, two_n, proj,
-    cot, cot_t, hid, rows, mas, one, two, old_ref, dest_ref,
+    cot, hid, rows, mas, one, two, old_ref, dest_ref,
     p_a, p_at, p_c, p_ct, p_s, p_st, own_a, own_b, slots, slots_u,
     ra1, ra1r, ra2, ra2r, rb1, rb1r, rb2, rb2r, row, rowx, rowp, rowq,
     ga0, ga0r, ga1, ga1r, ha, ha0, ha0r, ha1, ha1r,
@@ -266,6 +266,8 @@
     weight_a = weight_path(19, oa, da0, da1, wea)
     weight_b = weight_path(23, ob, db0, db1, web)
 
+    p_a[...] = reorder(3, 4, 2)
+
     in_copies[9].wait()
 
     dest = jnp.broadcast_to(dest_ref[...], (128, 128))
@@ -285,14 +287,14 @@
     pl.semaphore_wait(barrier, NY - 1 + NU - 1 + NX - 1)
     rows_a1[0]()
     rows_b1[0]()
-    p_a[...] = reorder(3, 4, 2)
 
     in_copies[0].wait()
-    cot_t[...] = cot[...].T
 
     def partial(b):
         in_copies[5 + b].wait()
-        return mm(cot_t[...], hid[:, b * 256 : (b + 1) * 256]).astype(BF)
+        return lax.dot_general(
+            cot[...], hid[:, b * 256 : (b + 1) * 256], (((0,), (0,)), ((), ())), preferred_element_type=F32
+        ).astype(BF)
 
     for b in range(2):
         lanes = slice(b * 128, (b + 1) * 128)
@@ -444,7 +446,7 @@
     v = lambda *s: pltpu.VMEM(s, BF)
     f = lambda *s: pltpu.VMEM(s, F32)
     scratch = [
-        v(1024, 512), v(512, 1024), v(1024, 1024), v(128, 512),
+        v(1024, 512), v(1024, 1024), v(128, 512),
         f(1024, 128), f(1024, 128), f(1024, 128), pltpu.VMEM((1, 128), I32), pltpu.VMEM((1, 128), I32),
         v(512, 512), v(512, 512), v(512, 512), v(512, 512), v(256, 256), v(256, 256),
         v(128, 512), v(128, 512), v(256, 128), v(256, 128),

time: 83.7 us -> 83 us (level)
  no operation moved by 1% of the time
where the time goes in v4:
time: 83 us; the launch traced here: 82.9 us
  Pallas kernels  81.6 us (98%)
  between operations  1.29 us (2%)
    pallas_call x1, Pallas kernels, body(): pl.pallas_call(kernel, out_shape=shapes, in_specs=[hbm, hbm, hbm, hbm, hb...  80.4 us

profile of v4, /device:TPU:1, one launch (start us, length us, event | category | flops | bytes accessed | tf_op | source)
XLA Modules:
  0.0 82.9 jit_solution(2264355664943455188)
XLA Ops:
  1.3 80.4 %whole_step.1 = (f32[1024,128]{1,0:T(8,128)S(1)}, f32[1024,128]{1,0:T(8,128)S(1)}, f32[1024,128]{1,0:T(8,128)S(1)}, bf16[128,256]{1,0:T(8,128)(2,1)S(1)}) custom-call(bf16[1024,512]{1,0:T(8,128)(2,1)} %cot_h.1, bf16[1024,1024]{1,0:T(8,128)(2,1)} %hid_h.1, s32[1,128]{1,0:T(1,128)} %bitcast.11, f32[1024,128]{1,0:T(8,128)} %bitcast.8, f32[1024,128]{1,0:T(8,128)} %bitcast.9, ...), custom_call_target="tpu_custom_call" | custom-call | tf_op jit(solution)/shard_map/whole_step/pallas_call | solution.py:470
  81.7 1.2 %commit.1 = (f32[1024,128]{1,0:T(8,128)}, f32[1024,128]{1,0:T(8,128)}, f32[1024,128]{1,0:T(8,128)}, bf16[128,256]{1,0:T(8,128)(2,1)}) custom-call(f32[1024,128]{1,0:T(8,128)S(1)} %get-tuple-element.12.a, f32[1024,128]{1,0:T(8,128)S(1)} %get-tuple-element.13.b, f32[1024,128]{1,0:T(8,128)S(1)} %get-tuple-element.14.c, bf16[128,256]{1,0:T(8,128)(2,1)S(1)} %get-tuple-element.15.d), custom_call_target="tpu_custom_call" | custom-call | tf_op jit(solution)/shard_map/commit/pallas_call | solution.py:485

commit v5 on v4

--- a/solution.py
+++ b/solution.py
@@ -380,12 +380,12 @@
     step(grad_b, gb1r, hb1r, 1, wb, cross_b[0])
     place_weights(cross_b[1], xb, yb, ob, weight_b[0])
 
+    weight_a[1]()
     sent.append(rows_a2[1]())
     row[:, :, :256] = ra2r[...]
     sent.append(rows_b2[1]())
     row[:, :, 256:] = mm(p_s[...], rb2r[...].reshape(256, 256)).astype(BF).reshape(NU, 16, 256)
     rowsx[0]()
-    weight_a[1]()
     weight_b[1]()
     sent.append(rowsx[1]())
     for b in range(4):

time: 83 us -> 82.8 us (level)
  no operation moved by 1% of the time
where the time goes in v5:
time: 82.8 us; the launch traced here: 82.7 us
  Pallas kernels  81.4 us (98%)
  between operations  1.29 us (2%)
    pallas_call x1, Pallas kernels, body(): pl.pallas_call(kernel, out_shape=shapes, in_specs=[hbm, hbm, hbm, hbm, hb...  80.2 us

profile of v5, /device:TPU:1, one launch (start us, length us, event | category | flops | bytes accessed | tf_op | source)
XLA Modules:
  0.0 82.7 jit_solution(13287835580535132184)
XLA Ops:
  1.3 80.2 %whole_step.1 = (f32[1024,128]{1,0:T(8,128)S(1)}, f32[1024,128]{1,0:T(8,128)S(1)}, f32[1024,128]{1,0:T(8,128)S(1)}, bf16[128,256]{1,0:T(8,128)(2,1)S(1)}) custom-call(bf16[1024,512]{1,0:T(8,128)(2,1)} %cot_h.1, bf16[1024,1024]{1,0:T(8,128)(2,1)} %hid_h.1, s32[1,128]{1,0:T(1,128)} %bitcast.11, f32[1024,128]{1,0:T(8,128)} %bitcast.8, f32[1024,128]{1,0:T(8,128)} %bitcast.9, ...), custom_call_target="tpu_custom_call" | custom-call | tf_op jit(solution)/shard_map/whole_step/pallas_call | solution.py:470
  81.5 1.2 %commit.1 = (f32[1024,128]{1,0:T(8,128)}, f32[1024,128]{1,0:T(8,128)}, f32[1024,128]{1,0:T(8,128)}, bf16[128,256]{1,0:T(8,128)(2,1)}) custom-call(f32[1024,128]{1,0:T(8,128)S(1)} %get-tuple-element.12.a, f32[1024,128]{1,0:T(8,128)S(1)} %get-tuple-element.13.b, f32[1024,128]{1,0:T(8,128)S(1)} %get-tuple-element.14.c, bf16[128,256]{1,0:T(8,128)(2,1)S(1)} %get-tuple-element.15.d), custom_call_target="tpu_custom_call" | custom-call | tf_op jit(solution)/shard_map/commit/pallas_call | solution.py:485
